TPU v7x, 32 devices: a whole 2x2x4 slice. The times are simulated.
32 devices in a mesh: dp: 2 (over x), expert: 8 (over z, y), tensor: 2 (over core).
Axes of the slice: x: 2, y: 2, z: 4, core: 2. Of those that a mesh axis runs over, the one named last changes fastest.
Arguments:
- activations: bfloat16 [4096, 1536], P(('dp', 'expert', 'tensor')), may hold values from -6 to 6
- segments: int32 [16, 256], P(('dp', 'expert')), may hold values from 0 to 3, never falling along the last dimension, each value on 1 to 128 neighbouring positions
- routes: int32 [4096, 8], P(('dp', 'expert', 'tensor')), may hold values from 0 to 15, all different within a row; in each aligned block of 128 rows (0 to 127, 128 to 255, ...) at most 128 rows name the same one
- route_weights: float32 [4096, 8], P(('dp', 'expert', 'tensor')), may hold values from 0.03 to 0.3
- norm_attn_gain: float32 [1536], replicated, may hold values from 0.5 to 1.5
- norm_ffn_gain: float32 [1536], replicated, may hold values from 0.5 to 1.5
- query_weight: bfloat16 [1536, 1536], P(None, 'tensor'), may hold values from -0.15625 to 0.15625
- key_matrix: bfloat16 [1536, 512], P(None, 'tensor'), may hold values from -0.15625 to 0.15625
- value_matrix: bfloat16 [1536, 512], P(None, 'tensor'), may hold values from -0.15625 to 0.15625
- output_projection_weight: bfloat16 [1536, 1536], P('tensor'), may hold values from -0.625 to 0.625
- expert_gate: bfloat16 [16, 1536, 512], P('expert', None, 'tensor'), may hold values from -0.15625 to 0.15625
- expert_up: bfloat16 [16, 1536, 512], P('expert', None, 'tensor'), may hold values from -0.15625 to 0.15625
- expert_down: bfloat16 [16, 512, 1536], P('expert', 'tensor'), may hold values from -0.5 to 0.5
- grad_output: bfloat16 [4096, 1536], P(('dp', 'expert', 'tensor')), may hold values from -6 to 6
Outputs:
- block_out: bfloat16 [4096, 1536], P(('dp', 'expert', 'tensor'))
- grad_input: float32 [4096, 1536], P(('dp', 'expert', 'tensor'))
- grad_norm_attn: float32 [1536], replicated
- grad_norm_ffn: float32 [1536], replicated
- grad_query: float32 [1536, 1536], P(None, 'tensor')
- grad_key: float32 [1536, 512], P(None, 'tensor')
- grad_value: float32 [1536, 512], P(None, 'tensor')
- grad_mixer: float32 [1536, 1536], P('tensor')
- grad_expert_gate: float32 [16, 1536, 512], P('expert', None, 'tensor')
- grad_expert_up: float32 [16, 1536, 512], P('expert', None, 'tensor')
- grad_expert_down: float32 [16, 512, 1536], P('expert', 'tensor')
Inputs may be any that keep to these rules, and one draw needn't show every extreme that they name: `routes`: each row names 8 different experts; in the rows of one device (aligned blocks of 128 rows) no expert is named more than 128 times, and one is named exactly 128 times in some block. `segments`: each sequence's numbers never fall; 4 documents of 1 to 128 positions, one of exactly 128.
All inputs are finite; a program needn't handle non-finite values.
Results may differ from a plain program's by a relative error of at most 0.01.
Values may be sent and summed in bfloat16 or wider, within the bound.
No kernel may reach another device: no remote copies, remote signals or barrier semaphores. Data moves between devices by JAX's collectives and lax.ppermute only.
A program may use at most 320 MiB of HBM per device.

v0:
```python
import jax
import jax.numpy as jnp
from jax import lax
from jax.sharding import PartitionSpec as P

HEAD_DIM = 64
EPS = 1e-05
ATTN_SCALE = 0.015625
THETA = 10000.0
NEG_FILL = -1e30
F32 = jnp.float32
BF16 = jnp.bfloat16


def swap(values):
    return lax.ppermute(values, "tensor", [(0, 1), (1, 0)])


def norm_forward(values, gain_vector):
    inv_scale = lax.rsqrt(jnp.mean(values * values, axis=-1, keepdims=True) + EPS)
    return (values * inv_scale * gain_vector, inv_scale)


def norm_backward(values, inv_scale, gain_vector, upstream):
    weighted = upstream * gain_vector
    inner = jnp.mean(weighted * values, axis=-1, keepdims=True)
    value_gradient = inv_scale * weighted - values * (inv_scale * inv_scale * inv_scale) * inner
    grad_gain = jnp.sum(upstream * values * inv_scale, axis=0)
    return (value_gradient, grad_gain)


def rope_tables(position):
    frequency = THETA ** (-jnp.arange(HEAD_DIM // 2, dtype=F32) * 2.0 / HEAD_DIM)
    angle_table = position.astype(F32)[:, None] * frequency[None, :]
    return (jnp.cos(angle_table)[:, None, :], jnp.sin(angle_table)[:, None, :])


def rotate(field_in, cosine, sine):
    first, second = jnp.split(field_in, 2, axis=-1)
    return jnp.concatenate(
        [first * cosine - second * sine, second * cosine + first * sine], axis=-1
    )


def dot(spec, left, right):
    return jnp.einsum(spec, left, right, preferred_element_type=F32)


def body(
    activations,
    segments,
    routes,
    route_weights,
    norm_attn_gain,
    norm_ffn_gain,
    query_weight,
    key_matrix,
    value_matrix,
    output_projection_weight,
    expert_gate,
    expert_up,
    expert_down,
    grad_output,
):
    tensor_rank = lax.axis_index("tensor")
    rows, width = activations.shape
    experts_here = expert_gate.shape[0]
    expert_count = experts_here * lax.axis_size("expert")
    length = segments.shape[1]
    heads_q = query_weight.shape[1] // HEAD_DIM
    heads_kv = key_matrix.shape[1] // HEAD_DIM
    group = heads_q // heads_kv
    position = (jnp.arange(length, dtype=jnp.int32) + tensor_rank * rows) % length
    seg_ids = jnp.where(tensor_rank == 0, segments[0], jnp.roll(segments[0], rows))
    cosine, sine = rope_tables(position)
    allowed = (position[None, :] <= position[:, None]) & (seg_ids[None, :] == seg_ids[:, None])
    gate = jnp.concatenate([expert_gate, swap(expert_gate)], axis=2)
    up = jnp.concatenate([expert_up, swap(expert_up)], axis=2)
    down = jnp.concatenate([expert_down, swap(expert_down)], axis=1)
    upstream_all = lax.all_gather(grad_output, "expert", axis=0, tiled=True)
    named = routes[:, :, None] == jnp.arange(expert_count, dtype=jnp.int32)
    weight_table = jnp.sum(jnp.where(named, route_weights[:, :, None], 0.0), axis=1)
    weights_all = lax.all_gather(weight_table, "expert", axis=0, tiled=True)
    first_expert = lax.axis_index("expert") * experts_here
    weights_here = lax.dynamic_slice_in_dim(weights_all, first_expert, experts_here, 1).T
    x_in = jnp.concatenate([activations, swap(activations)], axis=0).astype(F32)
    normed_one, scale_one = norm_forward(x_in, norm_attn_gain)
    hidden_first = normed_one.astype(BF16)
    queries = dot("td,da->ta", hidden_first, query_weight).reshape(length, heads_q, HEAD_DIM)
    queries = rotate(queries, cosine, sine).astype(BF16).reshape(length, heads_kv, group, HEAD_DIM)
    keys = dot("td,da->ta", hidden_first, key_matrix).reshape(length, heads_kv, HEAD_DIM)
    keys = rotate(keys, cosine, sine).astype(BF16)
    value_rows = dot("td,da->ta", hidden_first, value_matrix).astype(BF16)
    value_rows = value_rows.reshape(length, heads_kv, HEAD_DIM)
    scores = jnp.where(allowed, dot("qhgd,khd->hgqk", queries, keys) * ATTN_SCALE, NEG_FILL)
    top_score = jnp.max(scores, axis=-1, keepdims=True)
    log_total = top_score + jnp.log(jnp.sum(jnp.exp(scores - top_score), axis=-1, keepdims=True))
    mixed = dot("hgqk,khd->qhgd", jnp.exp(scores - log_total).astype(BF16), value_rows).astype(BF16)
    mixed_flat = mixed.reshape(length, heads_q * HEAD_DIM)
    attn_part = dot("ta,ad->td", mixed_flat, output_projection_weight)
    residual = x_in[:rows] + attn_part[:rows] + swap(attn_part[rows:])
    normed_two, scale_two = norm_forward(residual, norm_ffn_gain)
    tokens_in = lax.all_gather(normed_two.astype(BF16), "expert", axis=0, tiled=True)
    pre_gate = dot("td,edf->etf", tokens_in, gate)
    pre_up = dot("td,edf->etf", tokens_in, up)
    gate_sigmoid = jax.nn.sigmoid(pre_gate)
    activated = (pre_gate * gate_sigmoid * pre_up).astype(BF16)
    expert_out = dot("etf,efd->etd", activated, down).astype(BF16)
    mix_part = jnp.sum(weights_here[:, :, None] * expert_out.astype(F32), axis=0).astype(BF16)
    grad_rows = (weights_here[:, :, None] * upstream_all.astype(F32)[None]).astype(BF16)
    grad_act = dot("etd,efd->etf", grad_rows, down)
    grad_pre_gate = (
        grad_act * pre_up * gate_sigmoid * (1.0 + pre_gate * (1.0 - gate_sigmoid))
    ).astype(BF16)
    grad_pre_up = (grad_act * pre_gate * gate_sigmoid).astype(BF16)
    grad_in = dot("etf,edf->etd", grad_pre_gate, gate) + dot("etf,edf->etd", grad_pre_up, up)
    grad_part = jnp.sum(weights_here[:, :, None] * grad_in, axis=0).astype(BF16)
    grad_h_own = lax.psum_scatter(grad_part, "expert", scatter_dimension=0, tiled=True)
    expert_mix = lax.psum_scatter(mix_part, "expert", scatter_dimension=0, tiled=True)
    block_out = (residual + expert_mix.astype(F32)).astype(BF16)

    def expert_sum(whole, axis):
        own, other = jnp.split(whole, 2, axis=axis)
        half = own + swap(other.astype(BF16)).astype(F32)
        return lax.psum(half.astype(BF16), "dp").astype(F32)

    gate_sum = expert_sum(dot("td,etf->edf", tokens_in, grad_pre_gate), 2)
    up_sum = expert_sum(dot("td,etf->edf", tokens_in, grad_pre_up), 2)
    down_sum = expert_sum(dot("etf,etd->efd", activated, grad_rows), 1)
    upstream_own = grad_output.astype(F32)
    grad_norm_part, grad_ffn_gain = norm_backward(
        residual, scale_two, norm_ffn_gain, grad_h_own.astype(F32)
    )
    grad_resid = upstream_own + grad_norm_part
    resid_own = grad_resid.astype(BF16)
    resid_full = jnp.concatenate([resid_own, swap(resid_own)], axis=0)
    grad_mix_w = dot("sa,sb->ab", mixed_flat, resid_full)
    mixed_grad = dot("im,dm->id", resid_full, output_projection_weight).astype(BF16)
    mixed_grad = mixed_grad.reshape(length, heads_kv, group, HEAD_DIM)
    probs = jnp.exp(scores - log_total)
    row_delta = dot("qhgd,qhgd->hgq", mixed_grad, mixed)
    grad_soft = dot("qhgd,khd->hgqk", mixed_grad, value_rows)
    grad_scores = (probs * (grad_soft - row_delta[..., None]) * ATTN_SCALE).astype(BF16)
    grad_queries = dot("hgqk,khd->qhgd", grad_scores, keys)
    grad_keys = dot("hgqk,qhgd->khd", grad_scores, queries)
    grad_values = dot("hgqk,qhgd->khd", probs.astype(BF16), mixed_grad)
    grad_q_rows = rotate(grad_queries.reshape(length, heads_q, HEAD_DIM), cosine, -sine)
    grad_q_rows = grad_q_rows.astype(BF16).reshape(length, -1)
    grad_k_rows = rotate(grad_keys, cosine, -sine).astype(BF16).reshape(length, -1)
    grad_v_rows = grad_values.astype(BF16).reshape(length, -1)
    grad_q_w = dot("sd,sa->da", hidden_first, grad_q_rows)
    grad_k_w = dot("sd,sa->da", hidden_first, grad_k_rows)
    grad_v_w = dot("sd,sa->da", hidden_first, grad_v_rows)
    grad_h_part = (
        dot("sa,da->sd", grad_q_rows, query_weight)
        + dot("sa,da->sd", grad_k_rows, key_matrix)
        + dot("sa,da->sd", grad_v_rows, value_matrix)
    )
    grad_h_one = grad_h_part[:rows] + swap(grad_h_part[rows:])
    grad_x_part, grad_attn_gain = norm_backward(
        x_in[:rows], scale_one[:rows], norm_attn_gain, grad_h_one
    )
    grad_input = grad_resid + grad_x_part
    dense = [t.astype(BF16) for t in (grad_q_w, grad_k_w, grad_v_w, grad_mix_w)]
    dense = [t.astype(F32) for t in lax.psum(dense, ("dp", "expert"))]
    gains = lax.psum(jnp.stack([grad_attn_gain, grad_ffn_gain]), ("dp", "expert", "tensor"))
    return (block_out, grad_input, gains[0], gains[1], *dense, gate_sum, up_sum, down_sum)


def solution(mesh):
    tokens = P(("dp", "expert", "tensor"), None)
    whole = P()
    columns = P(None, "tensor")
    hidden_last = P("expert", None, "tensor")
    hidden_mid = P("expert", "tensor", None)
    mixer = P("tensor", None)
    return jax.shard_map(
        body,
        mesh=mesh,
        in_specs=(
            tokens,
            P(("dp", "expert"), None),
            tokens,
            tokens,
            whole,
            whole,
            columns,
            columns,
            columns,
            mixer,
            hidden_last,
            hidden_last,
            hidden_mid,
            tokens,
        ),
        out_specs=(
            tokens,
            tokens,
            whole,
            whole,
            columns,
            columns,
            columns,
            mixer,
            hidden_last,
            hidden_last,
            hidden_mid,
        ),
        check_vma=False,
    )
```

profile of v0, /device:TPU:0, one launch (start us, length us, event | category | flops | bytes accessed | tf_op | source)
XLA Modules:
  0.0 691.7 jit_solution(6405158610316332684)
XLA Ops:
  8.5 0.8 fusion.66
  10.9 0.8 fusion.43
  11.7 1.4 multiply_reduce_fusion.2
  13.1 1.8 fusion.64
  15.1 1.2 fusion.63
  18.4 1.0 copy-done.30
  20.0 0.9 convolution_convert_fusion.4
  20.9 0.8 fusion.67
  22.1 2.1 collective-permute-done.1
  25.5 0.9 multiply_convert_fusion.4
  26.6 2.6 copy.79
  29.6 2.6 copy.77
  32.3 32.2 %all_gather.9 = f32[1024,16]{0,1:T(8,128)S(1)} all-gather(f32[128,16]{0,1:T(8,128)S(1)} %select_reduce_fusion), channel_id=1, replica_groups=mesh['dp'=2,'expert'=8,'tensor'=2] {'expert'}, dimensions={0}, use_global_device_ids=true | all-gather | bytes 73728 | tf_op jit(solution)/shard_map/all_gather | solution.py:83
  64.6 2.7 constant_dynamic-update-slice_fusion.1
  67.2 2.7 constant_dynamic-update-slice_fusion
  69.9 4.5 all-gather.5.cloned.1.call-done
  74.3 5.4 convert_element_type.165
  79.7 56.4 %all-gather.3.cloned.1.call-done = bf16[1024,1536]{1,0:T(8,128)(2,1)} async-done(((bf16[128,1536]{1,0:T(8,128)(2,1)}), bf16[1024,1536]{1,0:T(8,128)(2,1)}) %all-gather.3.cloned.1.call-update) | async-done | bytes 3145744 | tf_op jit(solution)/shard_map/all_gather | solution.py:103
  136.1 6.9 %fusion.24 = f32[2,512,1024]{2,1,0:T(8,128)S(1)} fusion(bf16[1024,1536]{1,0:T(8,128)(2,1)} %all-gather.3.cloned.1.call-done, bf16[2,1536,256]{1,2,0:T(8,128)(2,1)} %collective-permute-done.3, bf16[2,1536,256]{1,2,0:T(8,128)(2,1)} %copy.79), kind=kOutput, calls=%fused_computation.46 | convolution fusion | flops 3227516928 | bytes 10485760 | tf_op jit(solution)/shard_map/td,edf->etf/dot_general | solution.py:46
  143.1 6.5 fusion.26
  149.7 9.5 %fusion.9 = (bf16[2,1024,512]{1,2,0:T(8,128)(2,1)}, bf16[2,1024,512]{1,2,0:T(8,128)(2,1)}, bf16[2,1024,512]{1,2,0:T(8,128)(2,1)S(1)}) fusion(f32[2,512,1024]{2,1,0:T(8,128)S(1)} %fusion.24, f32[2,512,1024]{2,1,0:T(8,128)} %fusion.26, bf16[2,512,1536]{2,1,0:T(8,128)(2,1)} %constant_dynamic-update-slice_fusion, f32[1024,1536]{1,0:T(8,128)S(1)} %bitcast.160, ...), kind=kOutput, calls=%fused_computation.16 | convolution fusion | flops 3244294144 | bytes 24125440 | tf_op jit(solution)/shard_map/etd,efd->etf/dot_general | solution.py:46
  159.1 8.6 %fusion.30 = f32[2,1024,1536]{2,1,0:T(8,128)} fusion(bf16[2,1024,512]{1,2,0:T(8,128)(2,1)S(1)} %get-tuple-element.61, bf16[2,1536,256]{1,2,0:T(8,128)(2,1)} %collective-permute-done.3, bf16[2,1536,256]{1,2,0:T(8,128)(2,1)S(1)} %copy-done.11), kind=kOutput, calls=%fused_computation.59 | convolution fusion | flops 3227516928 | bytes 17825792 | tf_op jit(solution)/shard_map/etf,edf->etd/dot_general | solution.py:46
  167.7 13.0 %multiply_reduce_fusion = bf16[1024,1536]{1,0:T(8,128)(2,1)} fusion(f32[2,1024,1536]{2,1,0:T(8,128)} %fusion.30, f32[2,1024]{1,0:T(2,128)S(1)} %dynamic-slice_bitcast_fusion, bf16[2,1024,512]{1,2,0:T(8,128)(2,1)} %get-tuple-element.59, bf16[2,1536,256]{1,2,0:T(8,128)(2,1)} %collective-permute-done.2, bf16[2,1536,256]{1,2,0:T(8,128)(2,1)} %copy.77), kind=kOutput, calls=%fused_computation | convolution fusion | flops 3235381248 | bytes 20979712 | tf_op jit(solution)/shard_map/etf,edf->etd/dot_general | solution.py:46
  181.0 7.1 %fusion = f32[2,512,1536]{2,1,0:T(8,128)S(1)} fusion(bf16[2,1024,512]{1,2,0:T(8,128)(2,1)} %get-tuple-element.60, f32[1024,1536]{1,0:T(8,128)} %convert_element_type.165, f32[2,1024]{1,0:T(2,128)S(1)} %dynamic-slice_bitcast_fusion), kind=kOutput, calls=%fused_computation.3 | convolution fusion | flops 3227516928 | bytes 14688256 | tf_op jit(solution)/shard_map/etf,etd->efd/dot_general | solution.py:46
  188.4 1.6 copy-done.62
  190.0 3.4 convolution_bitcast_fusion.1
  193.7 1.3 copy-done.65
  195.0 3.4 convolution_bitcast_fusion
  198.7 1.6 fusion.16
  200.3 1.8 fusion.18
  202.1 1.6 fusion.17
  203.8 8.9 %multiply_reduce_fusion.1 = bf16[1024,1536]{1,0:T(8,128)(2,1)} fusion(f32[2,1024]{1,0:T(2,128)S(1)} %dynamic-slice_bitcast_fusion, bf16[2,1024,512]{1,2,0:T(8,128)(2,1)} %get-tuple-element.60, bf16[2,512,1536]{2,1,0:T(8,128)(2,1)} %constant_dynamic-update-slice_fusion), kind=kOutput, calls=%fused_computation.2 | convolution fusion | flops 3232235520 | bytes 8396800 | tf_op jit(solution)/shard_map/etf,efd->etd/dot_general | solution.py:46
  212.9 41.2 %reduce-scatter.5.cloned.1.call-done = bf16[128,1536]{1,0:T(8,128)(2,1)} async-done(((bf16[1024,1536]{1,0:T(8,128)(2,1)}), bf16[128,1536]{1,0:T(8,128)(2,1)}) %reduce-scatter.5.cloned.1.call-update) | async-done | bytes 393232 | tf_op jit(solution)/shard_map/reduce_scatter | solution.py:118
  254.1 1.8 fusion.38
  256.0 1.4 fusion.62
  257.5 1.7 collective-permute-done.5
  259.9 1.6 convolution_convert_fusion.5
  261.5 2.0 copy.87
  263.4 1.1 fusion.40
  264.6 3.2 fusion.21
  269.7 1.4 convolution_convert_fusion.3
  271.5 0.8 fusion.31
  272.4 1.4 convolution_convert_fusion.2
  273.8 2.2 convolution_convert_fusion
  276.0 2.3 convolution_convert_fusion.1
  278.4 1.0 copy-done.19
  279.3 2.6 fusion.68
  283.5 1.1 copy-done.3
  284.7 0.9 slice.53
  287.1 88.6 %all-reduce.7.cloned.1.call-done = (bf16[2,1536,256]{1,2,0:T(8,128)(2,1)}, bf16[2,1536,256]{1,2,0:T(8,128)(2,1)}, bf16[2,256,1536]{2,1,0:T(8,128)(2,1)}) async-done(((bf16[2,1536,256]{1,2,0:T(8,128)(2,1)}, bf16[2,1536,256]{1,2,0:T(8,128)(2,1)}, bf16[2,256,1536]{2,1,0:T(8,128)(2,1)}), (bf16[2,1536,256]{1,2,0:T(8,128)(2,1)}, bf16[2,1536,256]{1,2,0:T(8,128)(2,1)}, ...) | async-done | bytes 4718608 | tf_op jit(solution)/shard_map/psum | solution.py:125
  375.8 3.1 copy.91
  378.8 3.1 copy.92
  381.9 3.6 convert_element_type.194
  385.6 1.9 multiply_reduce_fusion.3
  388.2 40.9 %psum.56 = f32[2,1536]{1,0:T(2,128)} all-reduce(f32[2,1536]{1,0:T(2,128)} %pad_maximum_fusion.14), channel_id=1, replica_groups=mesh['dp'=2,'expert'=8,'tensor'=2] {'dp','expert','tensor'}, use_global_device_ids=true, to_apply=%region_13.14 | all-reduce | flops 3072 | bytes 24576 | tf_op jit(solution)/shard_map/psum | solution.py:166
  429.0 1.4 slice_reduce_fusion
  430.4 1.2 broadcast_multiply_fusion
  431.6 24.1 %reduce-scatter.3.cloned.1.call-done = bf16[128,1536]{1,0:T(8,128)(2,1)} async-done(((bf16[1024,1536]{1,0:T(8,128)(2,1)}), bf16[128,1536]{1,0:T(8,128)(2,1)}) %reduce-scatter.3.cloned.1.call-update) | async-done | bytes 393232 | tf_op jit(solution)/shard_map/reduce_scatter | solution.py:119
  455.7 3.3 subtract_add_fusion
  459.0 216.4 %all-reduce.5.cloned.1.call-done = (bf16[1536,768]{1,0:T(8,128)(2,1)}, bf16[1536,256]{1,0:T(8,128)(2,1)}, bf16[1536,256]{1,0:T(8,128)(2,1)}, bf16[768,1536]{1,0:T(8,128)(2,1)}) async-done(((bf16[1536,768]{1,0:T(8,128)(2,1)}, bf16[1536,256]{1,0:T(8,128)(2,1)}, bf16[1536,256]{1,0:T(8,128)(2,1)}, bf16[768,1536]{1,0:T(8,128)(2,1)}), (bf16[1536,768]{1,0:T(8,128)(2,1)}, bf16[1536,256]{1,0:T(8,128)(2,1)}, ...) | async-done | bytes 6291472 | tf_op jit(solution)/shard_map/psum | solution.py:165
  675.5 2.5 convert_element_type.181
  678.0 1.3 convert_element_type.183
  679.3 2.5 convert_element_type.179
  681.8 2.8 convert_element_type.185
  (199 shorter events, 16.1 us)
Async XLA Ops:
  7.2 13.7 %copy-start = (bf16[768,1536]{1,0:T(8,128)(2,1)S(1)}, bf16[768,1536]{1,0:T(8,128)(2,1)}, u32[]{:S(2)}) copy-start(bf16[768,1536]{1,0:T(8,128)(2,1)} %param.23) | copy-start | bytes 7077892
  7.2 7.8 %copy-start.13 = (bf16[128,1536]{1,0:T(8,128)(2,1)S(1)}, bf16[128,1536]{1,0:T(8,128)(2,1)}, u32[]{:S(2)}) copy-start(bf16[128,1536]{1,0:T(8,128)(2,1)} %param.14) | copy-start | bytes 1179652
  7.2 7.8 %copy-start.46 = (f32[1536]{0:T(1024)S(1)}, f32[1536]{0:T(1024)}, u32[]{:S(2)}) copy-start(f32[1536]{0:T(1024)} %param.18) | copy-start | bytes 18436
  7.2 67.1 %all-gather.5.cloned.1.call-start = ((), (), s32[]{:S(2)}) async-start(), calls=%async_computation.4 | async-start | bytes 3538944 | tf_op jit(solution)/shard_map/all_gather | solution.py:80
  8.0 128.2 %all-gather.3.cloned.1.call-start = ((), (), s32[]{:S(2)}) async-start(), calls=%async_computation.2 | async-start | bytes 3538944 | tf_op jit(solution)/shard_map/all_gather | solution.py:103
  8.0 3.7 collective-permute-start
  8.5 6.5 copy-start.10
  10.9 9.1 %copy-start.41 = (pred[256,256]{0,1:T(8,128)(4,1)}, pred[256,256]{0,1:T(8,128)(4,1)S(1)}, u32[]{:S(2)}) copy-start(pred[256,256]{0,1:T(8,128)(4,1)S(1)} %compare_and_fusion) | copy-start | bytes 196612
  11.7 4.5 copy-start.22
  11.7 10.1 %copy-start.15 = (bf16[128,1536]{1,0:T(8,128)(2,1)}, bf16[128,1536]{1,0:T(8,128)(2,1)S(1)}, u32[]{:S(2)}) copy-start(bf16[128,1536]{1,0:T(8,128)(2,1)S(1)} %collective-permute-done) | copy-start | bytes 1179652
  13.1 5.3 copy-start.58
  16.4 2.0 copy-start.24
  17.7 2.3 copy-start.6
  17.7 1.7 copy-start.30
  21.8 3.7 copy-start.43
  21.8 2.4 collective-permute-start.1
  22.0 2.1 copy-start.1
  26.4 227.7 %reduce-scatter.5.cloned.1.call-start = ((), (), s32[]{:S(2)}) async-start(), calls=%async_computation.5 | async-start | bytes 3538944 | tf_op jit(solution)/shard_map/reduce_scatter | solution.py:118
  26.4 40.8 %collective-permute-start.4 = (bf16[2,256,1536]{2,1,0:T(8,128)(2,1)}, bf16[2,256,1536]{2,1,0:T(8,128)(2,1)}, u32[]{:S(2)}, u32[]{:S(2)}) collective-permute-start(bf16[2,256,1536]{2,1,0:T(8,128)(2,1)} %param.26), channel_id=1, source_target_pairs={{0,1},{1,0},{2,3},{3,2},{4,5},{5,4},{6,7},{7,6},{8,9},{9,8},{10,11... | collective-permute-start | bytes 4718600 | tf_op jit(solution)/shard_map/ppermute | solution.py:16
  29.2 3.1 copy-start.53
  29.2 3.1 copy-start.54
  29.2 50.5 %collective-permute-start.3 = (bf16[2,1536,256]{1,2,0:T(8,128)(2,1)}, bf16[2,1536,256]{1,2,0:T(8,128)(2,1)}, u32[]{:S(2)}, u32[]{:S(2)}) collective-permute-start(bf16[2,1536,256]{1,2,0:T(8,128)(2,1)} %copy.79), channel_id=1, source_target_pairs={{0,1},{1,0},{2,3},{3,2},{4,5},{5,4},{6,7},{7,6},{8,9},{9,8},{10,11... | collective-permute-start | bytes 4718600 | tf_op jit(solution)/shard_map/ppermute | solution.py:16
  32.2 110.9 %collective-permute-start.2 = (bf16[2,1536,256]{1,2,0:T(8,128)(2,1)}, bf16[2,1536,256]{1,2,0:T(8,128)(2,1)}, u32[]{:S(2)}, u32[]{:S(2)}) collective-permute-start(bf16[2,1536,256]{1,2,0:T(8,128)(2,1)} %copy.77), channel_id=1, source_target_pairs={{0,1},{1,0},{2,3},{3,2},{4,5},{5,4},{6,7},{7,6},{8,9},{9,8},{10,11... | collective-permute-start | bytes 4718600 | tf_op jit(solution)/shard_map/ppermute | solution.py:16
  136.1 7.0 %copy-start.12 = (bf16[2,1536,256]{1,2,0:T(8,128)(2,1)S(1)}, bf16[2,1536,256]{1,2,0:T(8,128)(2,1)}, u32[]{:S(2)}) copy-start(bf16[2,1536,256]{1,2,0:T(8,128)(2,1)} %copy.77) | copy-start | bytes 4718596
  136.1 7.0 %copy-start.61 = (bf16[1024,1536]{1,0:T(8,128)(2,1)S(1)}, bf16[1024,1536]{1,0:T(8,128)(2,1)}, u32[]{:S(2)}) copy-start(bf16[1024,1536]{1,0:T(8,128)(2,1)} %all-gather.3.cloned.1.call-done) | copy-start | bytes 9437188
  136.1 13.5 %slice-start = ((s8[6291456]{0:T(1024)(128)(4,1)}), s8[4194304]{0:T(1024)(128)(4,1)S(1)}, s32[]{:S(2)}) async-start(s8[6291456]{0:T(1024)(128)(4,1)} %bitcast.159), calls=%async_computation.8 | async-start | bytes 8388608
  143.1 6.6 slice-start.1
  149.6 9.5 %copy-start.11 = (bf16[2,1536,256]{1,2,0:T(8,128)(2,1)S(1)}, bf16[2,1536,256]{1,2,0:T(8,128)(2,1)}, u32[]{:S(2)}) copy-start(bf16[2,1536,256]{1,2,0:T(8,128)(2,1)} %copy.79) | copy-start | bytes 4718596
  159.1 8.6 %copy-start.64 = (bf16[2,1024,512]{1,2,0:T(8,128)(2,1)}, bf16[2,1024,512]{1,2,0:T(8,128)(2,1)S(1)}, u32[]{:S(2)}) copy-start(bf16[2,1024,512]{1,2,0:T(8,128)(2,1)S(1)} %get-tuple-element.61) | copy-start | bytes 6291460
  180.8 195.0 %all-reduce.7.cloned.1.call-start = ((), (), s32[]{:S(2)}) async-start(), calls=%async_computation.7 | async-start | bytes 9437184 | tf_op jit(solution)/shard_map/psum | solution.py:125
  181.0 7.3 %copy-start.66 = (bf16[2,1024,512]{1,2,0:T(8,128)(2,1)S(1)}, bf16[2,1024,512]{1,2,0:T(8,128)(2,1)}, u32[]{:S(2)}) copy-start(bf16[2,1024,512]{1,2,0:T(8,128)(2,1)} %get-tuple-element.59) | copy-start | bytes 6291460
  188.1 1.9 copy-start.62
  188.3 10.4 %collective-permute-start.9 = (bf16[2,256,1536]{2,1,0:T(8,128)(2,1)S(1)}, bf16[2,256,1536]{2,1,0:T(8,128)(2,1)S(1)}, u32[]{:S(2)}, u32[]{:S(2)}) collective-permute-start(bf16[2,256,1536]{2,1,0:T(8,128)(2,1)S(1)} %split.101), channel_id=1, source_target_pairs={{0,1},{1,0},{2,3},{3,2},{4,5},{5,4},{6,7},{7,6},{8,9},{9,8},{10,11... | collective-permute-start | bytes 4718600 | tf_op jit(solution)/shard_map/ppermute | solution.py:16
  193.4 1.6 copy-start.65
  193.6 6.7 collective-permute-start.7
  198.6 3.5 collective-permute-start.8
  203.7 252.0 %reduce-scatter.3.cloned.1.call-start = ((), (), s32[]{:S(2)}) async-start(), calls=%async_computation.3 | async-start | bytes 3538944 | tf_op jit(solution)/shard_map/reduce_scatter | solution.py:119
  212.6 41.5 %copy-start.52 = (f32[128]{0:T(128)S(1)}, f32[128]{0:T(128)}, u32[]{:S(2)}) copy-start(f32[128]{0:T(128)} %copy-done.51) | copy-start | bytes 1540
  212.6 43.3 %copy-start.56 = (f32[128]{0:T(128)S(1)}, f32[128]{0:T(128)}, u32[]{:S(2)}) copy-start(f32[128]{0:T(128)} %get-tuple-element.79) | copy-start | bytes 1540
  212.6 462.8 %all-reduce.5.cloned.1.call-start = ((), (), s32[]{:S(2)}) async-start(), calls=%async_computation.6 | async-start | bytes 12582912 | tf_op jit(solution)/shard_map/psum | solution.py:165
  257.4 1.8 copy-start.20
  257.4 1.8 collective-permute-start.5
  264.6 3.3 copy-start.25
  264.6 3.3 copy-start.27
  264.6 3.9 copy-start.23
  264.6 3.9 copy-start.36
  269.1 2.1 copy-start.7
  269.1 2.4 copy-start.17
  269.2 2.4 copy-start.42
  269.2 2.4 copy-start.50
  269.3 6.7 copy-start.18
  272.4 3.6 copy-start.44
  279.3 2.6 copy-start.29
  279.3 2.6 copy-start.33
  283.1 2.9 copy-start.60
  285.6 100.0 %collective-permute-start.6 = (f32[128,1536]{1,0:T(8,128)}, f32[128,1536]{1,0:T(8,128)}, u32[]{:S(2)}, u32[]{:S(2)}) collective-permute-start(f32[128,1536]{1,0:T(8,128)} %slice.53), channel_id=1, source_target_pairs={{0,1},{1,0},{2,3},{3,2},{4,5},{5,4},{6,7},{7,6},{8,9},{9,8},{10,11... | collective-permute-start | bytes 2359304 | tf_op jit(solution)/shard_map/ppermute | solution.py:16
  381.9 3.6 copy-start.48
  381.9 3.7 copy-start.2
  381.9 3.7 copy-start.4
  381.9 3.7 copy-start.55
  385.6 70.2 %copy-start.5 = (bf16[128,1536]{1,0:T(8,128)(2,1)S(1)}, bf16[128,1536]{1,0:T(8,128)(2,1)}, u32[]{:S(2)}) copy-start(bf16[128,1536]{1,0:T(8,128)(2,1)} %param.27) | copy-start | bytes 1179652
  675.5 2.5 copy-start.28
  675.5 3.8 copy-start.9
  679.3 2.5 copy-start.8
  (21 other events, 22.6 us)
Sparse Core Ops, SparseCore 0:
  10.2 64.0 all-gather.4
  77.1 58.9 all-gather.2
  180.9 73.1 reduce-scatter.4
  256.6 119.1 all-reduce.6
  380.2 75.4 reduce-scatter.2
  463.7 211.6 all-reduce.4
where the time goes:
time: 699 us; the launch traced here: 692 us
  waiting for transfers between devices  436 us (62%)
  matrix products  90.5 us (13%)
  blocking collectives  73.1 us (10%)
  other arithmetic  41.7 us (6%)
  local copies, waits for them, and re-layouts  32.8 us (5%)
  between operations  15.2 us (2%)
    psum x1, waiting for transfers between devices, body(): dense = [t.astype(F32) for t in lax.psum(dense, ('dp', 'expert'))]  216 us
    dot_general x27, matrix products, dot(): return jnp.einsum(spec, left, right, preferred_element_type=F32)  90.5 us
    psum x1, waiting for transfers between devices, expert_sum(): return lax.psum(half.astype(BF16), 'dp').astype(F32)  88.6 us
    all_gather x1, waiting for transfers between devices, body(): lax.all_gather(normed_two.astype(BF16), 'expert', axis=0, tiled=True)  56.4 us
    reduce_scatter x1, waiting for transfers between devices, body(): lax.psum_scatter(grad_part, 'expert', scatter_dimension=0, tiled=True)  41.2 us
    psum x1, blocking collectives, body(): lax.psum(jnp.stack([grad_attn_gain, grad_ffn_gain]), ('dp', 'expert', 'te...  40.9 us
    all_gather x1, blocking collectives, body(): weights_all = lax.all_gather(weight_table, 'expert', axis=0, tiled=True)  32.2 us
    reduce_scatter x1, waiting for transfers between devices, body(): lax.psum_scatter(mix_part, 'expert', scatter_dimension=0, tiled=True)  24.1 us
  transfers between devices with their start and end apart: 16, of which 8 were waited for; matrix products, arithmetic and copies ran while one was open for 16% of the time, Pallas kernels for 0%

commit v1 on v0

--- a/solution.py
+++ b/solution.py
@@ -1,3 +1,4 @@
+import functools
 import jax
 import jax.numpy as jnp
 from jax import lax
@@ -10,6 +11,14 @@
 NEG_FILL = -1e30
 F32 = jnp.float32
 BF16 = jnp.bfloat16
+
+
+def close_the_bands(u, across, peer_axis):
+    fresh = lax.psum(u, across)
+    return lax.psum(fresh, peer_axis)
+
+
+waves_see = functools.partial(close_the_bands, across="expert", peer_axis="dp")
 
 
 def swap(values):
@@ -162,7 +171,7 @@
     )
     grad_input = grad_resid + grad_x_part
     dense = [t.astype(BF16) for t in (grad_q_w, grad_k_w, grad_v_w, grad_mix_w)]
-    dense = [t.astype(F32) for t in lax.psum(dense, ("dp", "expert"))]
+    dense = [t.astype(F32) for t in waves_see(dense)]
     gains = lax.psum(jnp.stack([grad_attn_gain, grad_ffn_gain]), ("dp", "expert", "tensor"))
     return (block_out, grad_input, gains[0], gains[1], *dense, gate_sum, up_sum, down_sum)
 

time: 699 us -> 861 us (1.23)
  waiting for transfers between devices: 436 us -> 608 us
    psum x1, waiting for transfers between devices: 88.6 us -> 258 us  [expert_sum(): return lax.psum(half.astype(BF16), 'dp').astype(F32)]
    psum x1, waiting for transfers between devices: 216 us -> 181 us  [close_the_bands(): fresh = lax.psum(u, across)]
    reduce_scatter x1, waiting for transfers between devices: 41.2 us -> 73 us  [body(): lax.psum_scatter(grad_part, 'expert', scatter_dimension=0, tiled=True)]
    unnamed x143 -> x153, local copies, waits for them, and re-layouts: 23.8 us -> 22.1 us
  transfers between devices with their start and end apart: 16 -> 16, of which waited for: 8 -> 9; matrix products, arithmetic and copies ran while one was open for 16% -> 8% of each run, Pallas kernels for 0% -> 0%
where the time goes in v1:
time: 861 us; the launch traced here: 854 us
  waiting for transfers between devices  608 us (71%)
  matrix products  89.1 us (10%)
  blocking collectives  73.3 us (9%)
  other arithmetic  36.8 us (4%)
  local copies, waits for them, and re-layouts  27.9 us (3%)
  between operations  15.3 us (2%)
    psum x1, waiting for transfers between devices, expert_sum(): return lax.psum(half.astype(BF16), 'dp').astype(F32)  258 us
    psum x1, waiting for transfers between devices, close_the_bands(): fresh = lax.psum(u, across)  181 us
    dot_general x27, matrix products, dot(): return jnp.einsum(spec, left, right, preferred_element_type=F32)  89.1 us
    reduce_scatter x1, waiting for transfers between devices, body(): lax.psum_scatter(grad_part, 'expert', scatter_dimension=0, tiled=True)  73 us
    all_gather x1, waiting for transfers between devices, body(): lax.all_gather(normed_two.astype(BF16), 'expert', axis=0, tiled=True)  56.5 us
    psum x1, blocking collectives, body(): lax.psum(jnp.stack([grad_attn_gain, grad_ffn_gain]), ('dp', 'expert', 'te...  40.6 us
    all_gather x1, blocking collectives, body(): weights_all = lax.all_gather(weight_table, 'expert', axis=0, tiled=True)  32.7 us
    reduce_scatter x1, waiting for transfers between devices, body(): lax.psum_scatter(mix_part, 'expert', scatter_dimension=0, tiled=True)  28.9 us
  transfers between devices with their start and end apart: 16, of which 9 were waited for; matrix products, arithmetic and copies ran while one was open for 8% of the time, Pallas kernels for 0%

profile of v1, /device:TPU:0, one launch (start us, length us, event | category | flops | bytes accessed | tf_op | source)
XLA Modules:
  0.0 853.7 jit_solution(3887493215445191323)
XLA Ops:
  8.0 0.7 fusion.66
  8.7 0.8 broadcast_select_fusion
  9.5 0.7 and_select_fusion
  10.4 0.8 fusion.43
  11.2 1.4 multiply_reduce_fusion.2
  12.6 1.8 fusion.64
  14.6 1.2 fusion.63
  18.0 1.0 copy-done.33
  19.5 0.9 convolution_convert_fusion.4
  20.4 0.8 fusion.67
  21.6 2.1 collective-permute-done.1
  25.0 0.9 multiply_convert_fusion.4
  26.2 2.6 copy.77
  29.1 2.6 copy.79
  31.9 32.7 %all_gather.9 = f32[1024,16]{0,1:T(8,128)S(1)} all-gather(f32[128,16]{0,1:T(8,128)S(1)} %select_reduce_fusion), channel_id=1, replica_groups=mesh['dp'=2,'expert'=8,'tensor'=2] {'expert'}, dimensions={0}, use_global_device_ids=true | all-gather | bytes 73728 | tf_op jit(solution)/shard_map/all_gather | solution.py:92
  64.6 2.7 constant_dynamic-update-slice_fusion.1
  67.2 2.7 constant_dynamic-update-slice_fusion
  69.9 4.5 all-gather.5.cloned.1.call-done
  74.3 5.4 convert_element_type.165
  79.7 56.5 %all-gather.3.cloned.1.call-done = bf16[1024,1536]{1,0:T(8,128)(2,1)} async-done(((bf16[128,1536]{1,0:T(8,128)(2,1)}), bf16[1024,1536]{1,0:T(8,128)(2,1)}) %all-gather.3.cloned.1.call-update) | async-done | bytes 3145744 | tf_op jit(solution)/shard_map/all_gather | solution.py:112
  136.2 6.8 fusion.26
  143.1 6.5 fusion.24
  149.6 9.3 %fusion.9 = (bf16[2,1024,512]{1,2,0:T(8,128)(2,1)}, bf16[2,1024,512]{1,2,0:T(8,128)(2,1)}, bf16[2,1024,512]{1,2,0:T(8,128)(2,1)S(1)}) fusion(f32[2,512,1024]{2,1,0:T(8,128)} %fusion.24, f32[2,512,1024]{2,1,0:T(8,128)S(1)} %fusion.26, bf16[2,512,1536]{2,1,0:T(8,128)(2,1)} %constant_dynamic-update-slice_fusion, f32[1024,1536]{1,0:T(8,128)S(1)} %bitcast.160, ...), kind=kOutput, calls=%fused_computation.16 | convolution fusion | flops 3244294144 | bytes 24125440 | tf_op jit(solution)/shard_map/etd,efd->etf/dot_general | solution.py:55
  158.9 8.6 %fusion.30 = f32[2,1024,1536]{2,1,0:T(8,128)} fusion(bf16[2,1024,512]{1,2,0:T(8,128)(2,1)S(1)} %get-tuple-element.65, bf16[2,1536,256]{1,2,0:T(8,128)(2,1)} %collective-permute-done.3, bf16[2,1536,256]{1,2,0:T(8,128)(2,1)S(1)} %copy-done.13), kind=kOutput, calls=%fused_computation.59 | convolution fusion | flops 3227516928 | bytes 17825792 | tf_op jit(solution)/shard_map/etf,edf->etd/dot_general | solution.py:55
  167.5 13.0 %multiply_reduce_fusion = bf16[1024,1536]{1,0:T(8,128)(2,1)} fusion(f32[2,1024,1536]{2,1,0:T(8,128)} %fusion.30, f32[2,1024]{1,0:T(2,128)S(1)} %dynamic-slice_bitcast_fusion, bf16[2,1024,512]{1,2,0:T(8,128)(2,1)} %get-tuple-element.63, bf16[2,1536,256]{1,2,0:T(8,128)(2,1)} %collective-permute-done.2, bf16[2,1536,256]{1,2,0:T(8,128)(2,1)} %copy.77), kind=kOutput, calls=%fused_computation | convolution fusion | flops 3235381248 | bytes 20979712 | tf_op jit(solution)/shard_map/etf,edf->etd/dot_general | solution.py:55
  180.8 73.0 %reduce-scatter.5.cloned.1.call-done = bf16[128,1536]{1,0:T(8,128)(2,1)} async-done(((bf16[1024,1536]{1,0:T(8,128)(2,1)}), bf16[128,1536]{1,0:T(8,128)(2,1)}) %reduce-scatter.5.cloned.1.call-update) | async-done | bytes 393232 | tf_op jit(solution)/shard_map/reduce_scatter | solution.py:127
  253.8 1.8 fusion.38
  255.7 1.4 fusion.62
  257.2 1.7 collective-permute-done.5
  258.9 0.7 copy-done.37
  259.6 1.6 convolution_convert_fusion.5
  261.2 1.2 copy.87
  262.4 2.9 fusion.31
  265.5 1.1 fusion.21
  268.4 2.2 convolution_convert_fusion
  270.6 1.4 convolution_convert_fusion.2
  272.1 1.4 convolution_convert_fusion.3
  273.5 2.3 convolution_convert_fusion.1
  275.9 1.5 copy-done.12
  277.4 8.3 multiply_reduce_fusion.1
  286.0 6.5 fusion
  292.9 1.5 copy-done.66
  294.4 3.4 convolution_bitcast_fusion
  298.2 1.2 copy-done.71
  299.4 3.4 convolution_bitcast_fusion.1
  303.3 1.8 fusion.16
  305.0 1.7 fusion.17
  306.7 1.6 fusion.18
  308.4 181.1 %all-reduce.5.cloned.1.call-done = (bf16[1536,768]{1,0:T(8,128)(2,1)}, bf16[1536,256]{1,0:T(8,128)(2,1)}, bf16[1536,256]{1,0:T(8,128)(2,1)}, bf16[768,1536]{1,0:T(8,128)(2,1)}) async-done(((bf16[1536,768]{1,0:T(8,128)(2,1)}, bf16[1536,256]{1,0:T(8,128)(2,1)}, bf16[1536,256]{1,0:T(8,128)(2,1)}, bf16[768,1536]{1,0:T(8,128)(2,1)}), (bf16[1536,768]{1,0:T(8,128)(2,1)}, bf16[1536,256]{1,0:T(8,128)(2,1)}, ...) | async-done | bytes 6291472 | tf_op jit(solution)/shard_map/psum | solution.py:17
  489.5 1.0 copy-done.19
  490.5 2.6 fusion.68
  493.6 0.7 copy-done.34
  495.0 2.2 collective-permute-done.6
  498.1 40.6 %psum.84 = f32[2,1536]{1,0:T(2,128)S(1)} all-reduce(f32[2,1536]{1,0:T(2,128)S(1)} %pad_maximum_fusion.14), channel_id=1, replica_groups=mesh['dp'=2,'expert'=8,'tensor'=2] {'dp','expert','tensor'}, use_global_device_ids=true, to_apply=%region_13.14 | all-reduce | flops 3072 | bytes 24576 | tf_op jit(solution)/shard_map/psum | solution.py:175
  539.3 28.9 %reduce-scatter.3.cloned.1.call-done = bf16[128,1536]{1,0:T(8,128)(2,1)} async-done(((bf16[1024,1536]{1,0:T(8,128)(2,1)}), bf16[128,1536]{1,0:T(8,128)(2,1)}) %reduce-scatter.3.cloned.1.call-update) | async-done | bytes 393232 | tf_op jit(solution)/shard_map/reduce_scatter | solution.py:128
  568.3 2.9 subtract_add_fusion
  571.2 258.2 %all-reduce.7.cloned.1.call-done = (bf16[2,1536,256]{1,2,0:T(8,128)(2,1)}, bf16[2,1536,256]{1,2,0:T(8,128)(2,1)}, bf16[1536,768]{1,0:T(8,128)(2,1)}, bf16[1536,2...) async-done(((bf16[2,1536,256]{1,2,0:T(8,128)(2,1)}, bf16[2,1536,256]{1,2,0:T(8,128)(2,1)}, ...) | async-done | bytes 11010064 | tf_op jit(solution)/shard_map/psum | solution.py:134
  829.4 4.4 convert_element_type.179
  833.8 2.8 convert_element_type.185
  836.6 2.1 convert_element_type.194
  838.7 2.1 copy.91
  840.8 2.1 copy.92
  842.8 2.5 convert_element_type.181
  845.4 1.3 convert_element_type.183
  (209 shorter events, 12.6 us)
Async XLA Ops:
  7.2 13.2 %copy-start = (bf16[768,1536]{1,0:T(8,128)(2,1)S(1)}, bf16[768,1536]{1,0:T(8,128)(2,1)}, u32[]{:S(2)}) copy-start(bf16[768,1536]{1,0:T(8,128)(2,1)} %param.23) | copy-start | bytes 7077892
  7.2 7.3 copy-start.14
  7.2 7.3 copy-start.49
  7.2 67.1 %all-gather.5.cloned.1.call-start = ((), (), s32[]{:S(2)}) async-start(), calls=%async_computation.4 | async-start | bytes 3538944 | tf_op jit(solution)/shard_map/all_gather | solution.py:89
  7.3 4.0 collective-permute-start
  8.0 128.2 %all-gather.3.cloned.1.call-start = ((), (), s32[]{:S(2)}) async-start(), calls=%async_computation.2 | async-start | bytes 3538944 | tf_op jit(solution)/shard_map/all_gather | solution.py:112
  8.7 5.8 copy-start.11
  10.4 9.2 %copy-start.44 = (pred[256,256]{0,1:T(8,128)(4,1)}, pred[256,256]{0,1:T(8,128)(4,1)S(1)}, u32[]{:S(2)}) copy-start(pred[256,256]{0,1:T(8,128)(4,1)S(1)} %compare_and_fusion) | copy-start | bytes 196612
  11.2 4.5 copy-start.25
  11.2 10.2 %copy-start.16 = (bf16[128,1536]{1,0:T(8,128)(2,1)}, bf16[128,1536]{1,0:T(8,128)(2,1)S(1)}, u32[]{:S(2)}) copy-start(bf16[128,1536]{1,0:T(8,128)(2,1)S(1)} %collective-permute-done) | copy-start | bytes 1179652
  12.6 5.3 copy-start.62
  17.2 2.3 copy-start.7
  21.3 3.7 copy-start.46
  21.3 2.4 collective-permute-start.1
  21.6 2.1 copy-start.2
  25.9 227.9 %reduce-scatter.5.cloned.1.call-start = ((), (), s32[]{:S(2)}) async-start(), calls=%async_computation.5 | async-start | bytes 3538944 | tf_op jit(solution)/shard_map/reduce_scatter | solution.py:127
  26.0 41.3 %collective-permute-start.4 = (bf16[2,256,1536]{2,1,0:T(8,128)(2,1)}, bf16[2,256,1536]{2,1,0:T(8,128)(2,1)}, u32[]{:S(2)}, u32[]{:S(2)}) collective-permute-start(bf16[2,256,1536]{2,1,0:T(8,128)(2,1)} %param.26), channel_id=1, source_target_pairs={{0,1},{1,0},{2,3},{3,2},{4,5},{5,4},{6,7},{7,6},{8,9},{9,8},{10,11... | collective-permute-start | bytes 4718600 | tf_op jit(solution)/shard_map/ppermute | solution.py:25
  28.7 3.1 copy-start.57
  28.7 3.1 copy-start.58
  28.7 51.0 %collective-permute-start.2 = (bf16[2,1536,256]{1,2,0:T(8,128)(2,1)}, bf16[2,1536,256]{1,2,0:T(8,128)(2,1)}, u32[]{:S(2)}, u32[]{:S(2)}) collective-permute-start(bf16[2,1536,256]{1,2,0:T(8,128)(2,1)} %copy.77), channel_id=1, source_target_pairs={{0,1},{1,0},{2,3},{3,2},{4,5},{5,4},{6,7},{7,6},{8,9},{9,8},{10,11... | collective-permute-start | bytes 4718600 | tf_op jit(solution)/shard_map/ppermute | solution.py:25
  31.7 111.3 %collective-permute-start.3 = (bf16[2,1536,256]{1,2,0:T(8,128)(2,1)}, bf16[2,1536,256]{1,2,0:T(8,128)(2,1)}, u32[]{:S(2)}, u32[]{:S(2)}) collective-permute-start(bf16[2,1536,256]{1,2,0:T(8,128)(2,1)} %copy.79), channel_id=1, source_target_pairs={{0,1},{1,0},{2,3},{3,2},{4,5},{5,4},{6,7},{7,6},{8,9},{9,8},{10,11... | collective-permute-start | bytes 4718600 | tf_op jit(solution)/shard_map/ppermute | solution.py:25
  136.2 6.9 copy-start.13
  136.2 6.9 copy-start.65
  136.2 13.4 %slice-start = ((s8[6291456]{0:T(1024)(128)(4,1)}), s8[4194304]{0:T(1024)(128)(4,1)S(1)}, s32[]{:S(2)}) async-start(s8[6291456]{0:T(1024)(128)(4,1)} %bitcast.159), calls=%async_computation.8 | async-start | bytes 8388608
  143.0 6.6 slice-start.1
  158.9 8.6 %copy-start.69 = (bf16[2,1024,512]{1,2,0:T(8,128)(2,1)}, bf16[2,1024,512]{1,2,0:T(8,128)(2,1)S(1)}, u32[]{:S(2)}) copy-start(bf16[2,1024,512]{1,2,0:T(8,128)(2,1)S(1)} %get-tuple-element.65) | copy-start | bytes 6291460
  180.6 308.9 %all-reduce.5.cloned.1.call-start = ((), (), s32[]{:S(2)}) async-start(), calls=%async_computation.6 | async-start | bytes 12582912 | tf_op jit(solution)/shard_map/psum | solution.py:17
  257.1 1.8 copy-start.23
  257.1 1.8 collective-permute-start.5
  262.4 3.1 copy-start.8
  262.4 3.1 copy-start.45
  262.4 3.1 copy-start.54
  262.4 3.1 copy-start.68
  265.3 5.3 copy-start.47
  267.9 2.7 copy-start.15
  267.9 2.7 copy-start.17
  267.9 2.7 copy-start.50
  268.0 2.7 copy-start.63
  268.0 4.1 copy-start.35
  268.4 5.0 copy-start.18
  275.8 292.4 %reduce-scatter.3.cloned.1.call-start = ((), (), s32[]{:S(2)}) async-start(), calls=%async_computation.3 | async-start | bytes 3538944 | tf_op jit(solution)/shard_map/reduce_scatter | solution.py:128
  285.7 543.7 %all-reduce.7.cloned.1.call-start = ((), (), s32[]{:S(2)}) async-start(), calls=%async_computation.7 | async-start | bytes 22020096 | tf_op jit(solution)/shard_map/psum | solution.py:134
  286.0 6.9 copy-start.70
  292.5 1.9 copy-start.66
  292.7 10.6 %collective-permute-start.9 = (bf16[2,256,1536]{2,1,0:T(8,128)(2,1)S(1)}, bf16[2,256,1536]{2,1,0:T(8,128)(2,1)S(1)}, u32[]{:S(2)}, u32[]{:S(2)}) collective-permute-start(bf16[2,256,1536]{2,1,0:T(8,128)(2,1)S(1)} %split.101), channel_id=1, source_target_pairs={{0,1},{1,0},{2,3},{3,2},{4,5},{5,4},{6,7},{7,6},{8,9},{9,8},{10,11... | collective-permute-start | bytes 4718600 | tf_op jit(solution)/shard_map/ppermute | solution.py:25
  298.0 7.0 collective-permute-start.8
  303.0 3.8 collective-permute-start.7
  490.5 2.6 copy-start.32
  490.5 2.6 copy-start.36
  494.2 2.9 copy-start.3
  494.3 2.9 copy-start.51
  494.7 2.5 copy-start.4
  494.7 73.5 %copy-start.5 = (bf16[128,1536]{1,0:T(8,128)(2,1)S(1)}, bf16[128,1536]{1,0:T(8,128)(2,1)}, u32[]{:S(2)}) copy-start(bf16[128,1536]{1,0:T(8,128)(2,1)} %param.27) | copy-start | bytes 1179652
  494.7 73.5 %copy-start.6 = (bf16[128,1536]{1,0:T(8,128)(2,1)S(1)}, bf16[128,1536]{1,0:T(8,128)(2,1)}, u32[]{:S(2)}) copy-start(bf16[128,1536]{1,0:T(8,128)(2,1)} %reduce-scatter.5.cloned.1.call-done) | copy-start | bytes 1179652
  494.7 73.5 %copy-start.56 = (f32[128]{0:T(128)S(1)}, f32[128]{0:T(128)}, u32[]{:S(2)}) copy-start(f32[128]{0:T(128)} %copy-done.55) | copy-start | bytes 1540
  494.7 73.5 %copy-start.59 = (f32[128]{0:T(128)S(1)}, f32[128]{0:T(128)}, u32[]{:S(2)}) copy-start(f32[128]{0:T(128)} %get-tuple-element.83) | copy-start | bytes 1540
  494.8 73.5 %copy-start.61 = (f32[128]{0:T(128)S(1)}, f32[128]{0:T(128)}, u32[]{:S(2)}) copy-start(f32[128]{0:T(128)} %copy-done.60) | copy-start | bytes 1540
  494.8 2.4 collective-permute-start.6
  829.4 4.4 copy-start.10
  833.8 2.8 copy-start.22
  836.6 2.1 copy-start.21
  838.7 2.1 copy-start.20
  842.8 2.5 copy-start.31
  842.8 3.8 copy-start.1
  (26 other events, 30.4 us)
Sparse Core Ops, SparseCore 0:
  10.2 64.0 all-gather.4
  77.1 59.0 all-gather.2
  180.7 73.0 reduce-scatter.4
  275.9 213.5 all-reduce.4
  493.9 74.2 reduce-scatter.2
  572.6 256.7 all-reduce.6
